TPU v7x, 32 devices: a whole 2x2x4 slice. The times are simulated.
32 devices in a mesh: chan: 4 (over y, core), seq: 8 (over z, x).
Axes of the slice: x: 2, y: 2, z: 4, core: 2. Of those that a mesh axis runs over, the one named last changes fastest.
Arguments:
- query_proj: bfloat16 [65536, 2048], P('seq', 'chan'), may hold values from -6 to 6
- key_proj: bfloat16 [65536, 2048], P('seq', 'chan'), may hold values from -6 to 6
- value_proj: bfloat16 [65536, 2048], P('seq', 'chan'), may hold values from -6 to 6
- short_taps: float32 [3, 3, 2048], P(None, None, 'chan'), may hold values from -3.5 to 3.5
- skip_gain: float32 [2048], P('chan'), may hold values from -6 to 6
- long_filter: float32 [4, 65536], P('chan', 'seq'), may hold values from -0.0234375 to 0.0234375
Outputs:
- mixed: float32 [65536, 2048], P('seq', 'chan')
All inputs are finite; a program needn't handle non-finite values.
Results may differ from a plain program's by a relative error of at most 0.0003.
Values may be sent and summed in bfloat16 or wider, within the bound.
No kernel may reach another device: no remote copies, remote signals or barrier semaphores. Data moves between devices by JAX's collectives and lax.ppermute only.
A program may use at most 256 MiB of HBM per device.

v0:
```python
from functools import partial
import math
import jax
import jax.numpy as jnp
from jax import lax
from jax.sharding import PartitionSpec as P

A = 256
B = 256
EXACT = lax.Precision.HIGHEST


def from_behind(value, axis, steps):
    count = lax.axis_size(axis)
    initial, last = (max(0, -steps), min(count, count - steps))
    return lax.ppermute(value, axis, [(source, source + steps) for source in range(initial, last)])


def phase_table(count_rows, count_cols, period, col_start):
    row_index = lax.broadcasted_iota(jnp.int32, (count_rows, count_cols), 0)
    col_index = lax.broadcasted_iota(jnp.int32, (count_rows, count_cols), 1) + col_start
    residue = row_index * col_index % period
    angle_val = 2.0 * math.pi / period * residue.astype(jnp.float32)
    return (jnp.cos(angle_val), jnp.sin(angle_val))


def complex_apply(pattern, matrix_re, matrix_im, data_re, data_im):
    product = partial(jnp.einsum, pattern, precision=EXACT)
    if data_im is None:
        return (product(matrix_re, data_re), product(matrix_im, data_re))
    return (
        product(matrix_re, data_re) - product(matrix_im, data_im),
        product(matrix_re, data_im) + product(matrix_im, data_re),
    )


def complex_times(first_re, first_im, second_re, second_im):
    return (
        first_re * second_re - first_im * second_im,
        first_re * second_im + first_im * second_re,
    )


def lane_forward(block, twiddle_re, twiddle_im):
    cos_b, sin_b = phase_table(B, B, B, 0)
    inner_re, inner_im = complex_apply("kb,bam->kam", cos_b, -sin_b, block[:, :, 0], block[:, :, 1])
    return complex_times(inner_re, inner_im, twiddle_re[:, :, None], -twiddle_im[:, :, None])


def lane_spectrum(block):
    cos_a, sin_a = phase_table(A, A, A, 0)
    return complex_apply("ja,kam->kjm", cos_a, -sin_a, block[:, :, 0], block[:, :, 1])


def lane_unspectrum(spec_re, spec_im):
    cos_a, sin_a = phase_table(A, A, A, 0)
    return complex_apply("ja,kjm->kam", cos_a, sin_a, spec_re, spec_im)


def lane_backward(block, twiddle_re, twiddle_im):
    turned_re, turned_im = complex_times(
        block[:, :, 0], block[:, :, 1], twiddle_re[:, :, None], twiddle_im[:, :, None]
    )
    cos_b, sin_b = phase_table(B, B, B, 0)
    out_re, out_im = complex_apply("kb,kam->bam", cos_b, sin_b, turned_re, turned_im)
    factor = 1.0 / (A * B)
    return (out_re * factor, out_im * factor)


def per_device(query_proj, key_proj, value_proj, short_taps, skip_gain, long_filter):
    tok_count, chan_width = query_proj.shape
    previous = from_behind((query_proj[-2:], key_proj[-2:], value_proj[-2:]), "seq", 1)

    def depthwise(signal, before, column):
        padded = jnp.concatenate([before, signal], axis=0).astype(jnp.float32)
        return (
            short_taps[0, column] * padded[2:]
            + short_taps[1, column] * padded[1:-1]
            + short_taps[2, column] * padded[:-2]
        )

    query_short = depthwise(query_proj, previous[0], 0)
    key_short = depthwise(key_proj, previous[1], 1)
    value_short = depthwise(value_proj, previous[2], 2)
    gated = key_short * value_short
    seq_count = lax.axis_size("seq")
    low_count = A // seq_count
    high_count = tok_count // A
    half_width = chan_width // 2
    signal_block = gated.reshape(high_count, A, 2, half_width)
    filter_taps_local = long_filter.reshape(high_count, A, 1, 1)
    filter_block = jnp.concatenate([filter_taps_local, jnp.zeros_like(filter_taps_local)], axis=2)
    signal_block, filter_block = (
        lax.all_to_all(signal_block, "seq", split_axis=1, concat_axis=0, tiled=True),
        lax.all_to_all(filter_block, "seq", split_axis=1, concat_axis=0, tiled=True),
    )
    position = lax.axis_index("seq")
    twiddle_re, twiddle_im = phase_table(B, low_count, A * B, position * low_count)
    sig_re, sig_im = lane_forward(signal_block, twiddle_re, twiddle_im)
    fil_re, fil_im = lane_forward(filter_block, twiddle_re, twiddle_im)
    signal_block, filter_block = (
        lax.all_to_all(
            jnp.stack([sig_re, sig_im], axis=2), "seq", split_axis=0, concat_axis=1, tiled=True
        ),
        lax.all_to_all(
            jnp.stack([fil_re, fil_im], axis=2), "seq", split_axis=0, concat_axis=1, tiled=True
        ),
    )
    freq_re, freq_im = lane_spectrum(signal_block)
    spectrum_re, spectrum_im = lane_spectrum(filter_block)
    mult_re, mult_im = complex_times(freq_re, freq_im, spectrum_re, spectrum_im)
    back_re, back_im = lane_unspectrum(mult_re, mult_im)
    back_block = lax.all_to_all(
        jnp.stack([back_re, back_im], axis=2), "seq", split_axis=1, concat_axis=0, tiled=True
    )
    conv_re, conv_im = lane_backward(back_block, twiddle_re, twiddle_im)
    convolved = lax.all_to_all(
        jnp.stack([conv_re, conv_im], axis=2), "seq", split_axis=0, concat_axis=1, tiled=True
    )
    convolved = convolved.reshape(tok_count, chan_width)
    return query_short * (convolved + skip_gain * gated)


def solution(mesh):
    return jax.shard_map(
        per_device,
        mesh=mesh,
        in_specs=(
            P("seq", "chan"),
            P("seq", "chan"),
            P("seq", "chan"),
            P(None, None, "chan"),
            P("chan"),
            P("chan", "seq"),
        ),
        out_specs=P("seq", "chan"),
        check_vma=False,
    )
```

profile of v0, /device:TPU:20, one launch (start us, length us, event | category | flops | bytes accessed | tf_op | source)
XLA Modules:
  0.0 2002.1 jit_solution(7467788233628211995)
XLA Ops:
  0.7 3.4 collective-permute-start.1
  4.8 3.4 collective-permute-start.2
  10.1 5.1 all-to-all-start.2
  15.3 1.6 fusion.195
  16.8 10.3 maximum_convert_fusion.1
  27.2 6.3 maximum_convert_fusion.2
  33.5 39.5 %fusion.1 = f32[8192,512]{1,0:T(8,128)} fusion(f32[8194,512]{1,0:T(8,128)} %maximum_convert_fusion.2, f32[8194,512]{1,0:T(8,128)} %maximum_convert_fusion.1, f32[512]{0:T(512)S(1)} %bitcast.234, f32[512]{0:T(512)S(1)} %bitcast.235, f32[512]{0:T(512)S(1)} %bitcast.230, f32[512]{0:T(512)S(1)} %bitcast.231, f32[512]{0:T(512)S(1)} %bitcast.232, f32[512]{0:T(512)S(1)} %bitcast.233), kind=kLoop, calls=%fused_computation.2 | loop fusion | flops 46137344 | bytes 117452800 | tf_op jit(solution)/shard_map/mul | solution.py:85
  73.0 19.9 reshape.143
  92.9 17.7 copy.125
  110.6 6.3 all-to-all-start
  122.6 1.9 fusion.96
  127.1 348.4 %all-to-all-done = f32[32,256,2,256]{3,0,2,1:T(8,128)} async-done(((f32[32,256,2,256]{3,0,2,1:T(8,128)}), f32[32,256,2,256]{3,0,2,1:T(8,128)}, u32[]{:S(2)}, u32[]{:S(2)}) %all-to-all-start) | async-done | bytes 16777248 | tf_op jit(solution)/shard_map/all_to_all | solution.py:94
  475.5 7.4 all-to-all-start.3
  482.9 6.6 copy.127
  489.5 11.7 fusion.16
  501.2 11.6 fusion.17
  512.8 11.8 fusion.19
  524.7 21.5 %subtract_bitcast_fusion.1 = (f32[256,32,1,256]{3,0,1,2:T(8,128)}, f32[256,32,1,256]{3,0,1,2:T(8,128)}) fusion(f32[256,32]{0,1:T(8,128)S(1)} %get-tuple-element.21, f32[256,32]{0,1:T(8,128)S(1)} %get-tuple-element.24, f32[256,32,256]{2,0,1:T(8,128)} %fusion.16, f32[256,32,256]{2,0,1:T(8,128)} %fusion.17, f32[256,32,256]{2,0,1:T(8,128)} %fusion.19, ...), kind=kOutput, calls=%fused_computation.46 | convolution fusion | flops 6460145664 | bytes 50397184 | tf_op jit(solution)/shard_map/kb,bam->kam/dot_general | solution.py:33
  546.2 6.9 pad_maximum_fusion
  553.1 20.2 %copy.132 = f32[256,32,2,256]{3,1,2,0:T(8,128)} copy(f32[256,32,2,256]{3,0,1,2:T(8,128)S(1)} %pad_maximum_fusion) | data formatting | bytes 33554432 | tf_op jit(solution)/shard_map/stack | solution.py:103
  573.3 6.0 all-to-all-start.1
  585.8 352.9 %all-to-all-done.1 = f32[256,32,2,256]{3,1,2,0:T(8,128)} async-done(((f32[256,32,2,256]{3,1,2,0:T(8,128)}), f32[256,32,2,256]{3,1,2,0:T(8,128)}, u32[]{:S(2)}, u32[]{:S(2)}) %all-to-all-start.1) | async-done | bytes 16777248 | tf_op jit(solution)/shard_map/all_to_all | solution.py:102
  938.7 6.6 copy.133
  945.3 18.3 fusion.20
  963.6 18.0 fusion.21
  981.6 18.1 fusion.23
  999.7 25.9 %multiply_subtract_fusion.1 = (f32[32,256,256]{2,1,0:T(8,128)}, f32[32,256,256]{2,1,0:T(8,128)}) fusion(f32[32,256]{1,0:T(8,128)S(1)} %convolution_add_fusion, f32[32,256]{1,0:T(8,128)S(1)} %convolution_subtract_fusion, f32[32,256,256]{2,1,0:T(8,128)} %fusion.20, f32[32,256,256]{2,1,0:T(8,128)} %fusion.21, f32[32,256,256]{2,1,0:T(8,128)} %fusion.23, ...), kind=kOutput, calls=%fused_computation.44 | convolution fusion | flops 6460145664 | bytes 50397184 | tf_op jit(solution)/shard_map/ja,kam->kjm/dot_general | solution.py:33
  1025.7 13.4 fusion.10
  1039.1 7.7 fusion.8
  1046.8 11.3 subtract_bitcast_fusion
  1058.0 10.9 add_bitcast_fusion
  1068.9 9.8 pad_maximum_fusion.1
  1078.7 19.9 copy.149
  1098.6 368.1 %all_to_all.105 = f32[32,256,2,256]{3,0,2,1:T(8,128)S(1)} all-to-all(f32[32,256,2,256]{3,0,2,1:T(8,128)} %copy.149), channel_id=1, replica_groups=mesh['chan'=4,'seq'=8] {'seq'}, dimensions={1} | all-to-all | bytes 33554432 | tf_op jit(solution)/shard_map/all_to_all | solution.py:113
  1466.7 2.1 copy.151
  1468.8 12.5 fusion.28
  1481.2 12.6 fusion.29
  1493.9 17.5 multiply_bitcast_fusion.1
  1511.4 16.1 multiply_bitcast_fusion
  1527.4 6.9 pad_maximum_fusion.2
  1534.3 20.3 %copy.152 = f32[256,32,2,256]{3,1,2,0:T(8,128)} copy(f32[256,32,2,256]{3,0,1,2:T(8,128)S(1)} %pad_maximum_fusion.2) | data formatting | bytes 33554432 | tf_op jit(solution)/shard_map/stack | solution.py:118
  1554.7 8.1 all-to-all-start.5
  1563.5 3.4 collective-permute-start
  1566.9 356.4 %collective-permute-done = bf16[2,512]{1,0:T(2,128)(2,1)S(1)} collective-permute-done((bf16[2,512]{1,0:T(2,128)(2,1)S(1)}, bf16[2,512]{1,0:T(2,128)(2,1)S(1)}, u32[]{:S(2)}, u32[]{:S(2)}) %collective-permute-start) | collective-permute-done | bytes 2080 | tf_op jit(solution)/shard_map/ppermute | solution.py:16
  1923.2 9.8 maximum_convert_fusion
  1933.1 27.6 %copy.153 = f32[32,8,32,2,256]{4,3,2,1,0:T(2,128)S(1)} copy(f32[32,8,32,2,256]{4,2,3,0,1:T(8,128)} %bitcast.62) | data formatting | bytes 33554432 | tf_op jit(solution)/shard_map/all_to_all | solution.py:117
  1960.7 7.2 copy.187
  1968.0 33.7 %fusion.6 = f32[8192,512]{1,0:T(8,128)} fusion(f32[8194,512]{1,0:T(8,128)} %maximum_convert_fusion, f32[8192,512]{1,0:T(8,128)} %bitcast.215, f32[8192,512]{1,0:T(8,128)} %fusion.1, f32[512]{0:T(512)S(1)} %copy-done.9, f32[512]{0:T(512)S(1)} %bitcast.228, f32[512]{0:T(512)S(1)} %bitcast.229, f32[512]{0:T(512)S(1)} %bitcast.227), kind=kLoop, calls=%fused_computation.13 | loop fusion | flops 33554432 | bytes 100671488 | tf_op jit(solution)/shard_map/mul | solution.py:121
  (63 shorter events, 18.8 us)
Async XLA Ops:
  0.7 16.1 collective-permute-start.1
  4.8 22.4 %collective-permute-start.2 = (bf16[2,512]{1,0:T(2,128)(2,1)S(1)}, bf16[2,512]{1,0:T(2,128)(2,1)S(1)}, u32[]{:S(2)}, u32[]{:S(2)}) collective-permute-start(bf16[2,512]{1,0:T(2,128)(2,1)S(1)} %slice.108), channel_id=1, source_target_pairs={{0,1},{1,2},{2,3},{3,4},{4,5},{5,6},{6,7},{8,9},{9,10},{10,11},{11... | collective-permute-start | bytes 6152 | tf_op jit(solution)/shard_map/ppermute | solution.py:16
  10.1 100.4 %all-to-all-start.2 = ((f32[8,1,2048]{2,1,0:T(1,128)}), f32[8,1,2048]{2,1,0:T(1,128)S(1)}, u32[]{:S(2)}, u32[]{:S(2)}) async-start(f32[8,1,2048]{2,1,0:T(1,128)} %reshape.153), calls=%async_computation.2 | async-start | bytes 131072 | tf_op jit(solution)/shard_map/all_to_all | solution.py:95
  15.3 11.9 slice-start.2
  16.8 10.4 slice-start.3
  110.6 364.9 %all-to-all-start = ((f32[32,256,2,256]{3,0,2,1:T(8,128)}), f32[32,256,2,256]{3,0,2,1:T(8,128)}, u32[]{:S(2)}, u32[]{:S(2)}) async-start(f32[32,256,2,256]{3,0,2,1:T(8,128)} %copy.125), calls=%async_computation | async-start | bytes 33554432 | tf_op jit(solution)/shard_map/all_to_all | solution.py:94
  475.5 97.8 %all-to-all-start.3 = ((f32[8,1,2048]{2,1,0:T(1,128)}), f32[8,1,2048]{2,1,0:T(1,128)S(1)}, u32[]{:S(2)}, u32[]{:S(2)}) async-start(f32[8,1,2048]{2,1,0:T(1,128)} %reshape.155), calls=%async_computation.3 | async-start | bytes 131072 | tf_op jit(solution)/shard_map/all_to_all | solution.py:105
  489.5 23.3 %copy-start.2 = (f32[8,32,32,2,256]{4,1,0,2,3:T(8,128)}, f32[8,32,32,2,256]{4,1,0,2,3:T(8,128)S(1)}, u32[]{:S(2)}) copy-start(f32[8,32,32,2,256]{4,1,0,2,3:T(8,128)S(1)} %copy.127) | copy-start | bytes 50331652
  573.3 365.4 %all-to-all-start.1 = ((f32[256,32,2,256]{3,1,2,0:T(8,128)}), f32[256,32,2,256]{3,1,2,0:T(8,128)}, u32[]{:S(2)}, u32[]{:S(2)}) async-start(f32[256,32,2,256]{3,1,2,0:T(8,128)} %copy.132), calls=%async_computation.1 | async-start | bytes 33554432 | tf_op jit(solution)/shard_map/all_to_all | solution.py:102
  945.3 36.3 %copy-start.1 = (f32[32,8,32,2,256]{4,2,1,3,0:T(8,128)}, f32[32,8,32,2,256]{4,2,1,3,0:T(8,128)S(1)}, u32[]{:S(2)}) copy-start(f32[32,8,32,2,256]{4,2,1,3,0:T(8,128)S(1)} %copy.133) | copy-start | bytes 50331652
  1025.7 13.4 copy-start.3
  1025.7 21.1 %slice-start = ((s8[8388608]{0:T(1024)(128)(4,1)}), s8[4194304]{0:T(1024)(128)(4,1)S(1)}, s32[]{:S(2)}) async-start(s8[8388608]{0:T(1024)(128)(4,1)} %bitcast.213), calls=%async_computation.6 | async-start | bytes 8388608
  1039.1 7.7 slice-start.1
  1466.7 2.1 copy-start.5
  1468.7 12.5 copy-start
  1493.9 17.5 copy-start.4
  1554.7 378.4 %all-to-all-start.5 = ((f32[256,32,2,256]{3,1,2,0:T(8,128)}), f32[256,32,2,256]{3,1,2,0:T(8,128)}, u32[]{:S(2)}, u32[]{:S(2)}) async-start(f32[256,32,2,256]{3,1,2,0:T(8,128)} %copy.152), calls=%async_computation.5 | async-start | bytes 33554432 | tf_op jit(solution)/shard_map/all_to_all | solution.py:117
  1563.5 359.7 %collective-permute-start = (bf16[2,512]{1,0:T(2,128)(2,1)S(1)}, bf16[2,512]{1,0:T(2,128)(2,1)S(1)}, u32[]{:S(2)}, u32[]{:S(2)}) collective-permute-start(bf16[2,512]{1,0:T(2,128)(2,1)S(1)} %slice.94), channel_id=1, source_target_pairs={{0,1},{1,2},{2,3},{3,4},{4,5},{5,6},{6,7},{8,9},{9,10},{10,11},{11... | collective-permute-start | bytes 6152 | tf_op jit(solution)/shard_map/ppermute | solution.py:16
  1960.7 7.3 copy-start.6
  1960.7 7.3 copy-start.7
  1960.7 7.3 copy-start.8
  1960.7 7.3 copy-start.9
where the time goes:
time: 2010 us; the launch traced here: 2000 us
  waiting for transfers between devices  1060 us (53%)
  blocking collectives  368 us (18%)
  matrix products  249 us (12%)
  local copies, waits for them, and re-layouts  157 us (8%)
  other arithmetic  126 us (6%)
  starting transfers between devices  43.1 us (2%)
    all_to_all x1, blocking collectives, per_device(): lax.all_to_all(jnp.stack([back_re, back_im], axis=2), 'seq', split_axis=1...  368 us
    ppermute x3, waiting for transfers between devices, from_behind(): lax.ppermute(value, axis, [(source, source + steps) for source in range(i...  356 us
    all_to_all x1, waiting for transfers between devices, per_device(): lax.all_to_all(jnp.stack([sig_re, sig_im], axis=2), 'seq', split_axis=0,...  353 us
    all_to_all x1, waiting for transfers between devices, per_device(): lax.all_to_all(signal_block, 'seq', split_axis=1, concat_axis=0, tiled=True)  348 us
    dot_general x6, matrix products, complex_apply(): product(matrix_re, data_im) + product(matrix_im, data_re)  70.2 us
    dot_general x6, matrix products, complex_apply(): product(matrix_im, data_im)  64 us
    dot_general x6, matrix products, complex_apply(): product(matrix_im, data_re)  59.5 us
    dot_general x6, matrix products, complex_apply(): product(matrix_re, data_re) - product(matrix_im, data_im)  55.7 us
  transfers between devices with their start and end apart: 8, of which 3 were waited for; matrix products, arithmetic and copies ran while one was open for 11% of the time, Pallas kernels for 0%

commit v1 on v0

--- a/solution.py
+++ b/solution.py
@@ -8,6 +8,30 @@
 A = 256
 B = 256
 EXACT = lax.Precision.HIGHEST
+
+
+def split_up(x, dim, size):
+    shape = x.shape
+    blocks = x.reshape(*shape[:dim], size, shape[dim] // size, *shape[dim + 1 :])
+    return jnp.moveaxis(blocks, dim, 0)
+
+
+def in_order(blocks, dim):
+    blocks = jnp.moveaxis(blocks, 0, dim)
+    shape = blocks.shape
+    return blocks.reshape(*shape[:dim], shape[dim] * shape[dim + 1], *shape[dim + 2 :])
+
+
+def sent_to_each(x, axis, split_dim, concat_dim):
+    devices, mine = (lax.axis_size(axis), lax.axis_index(axis))
+    parts = split_up(x, split_dim, devices)
+    out = parts
+    for hop in range(1, devices):
+        target, source = ((mine + hop) % devices, (mine - hop) % devices)
+        sent = lax.dynamic_index_in_dim(parts, target, 0)
+        partner_block = lax.ppermute(sent, axis, [(i, (i + hop) % devices) for i in range(devices)])
+        out = lax.dynamic_update_slice_in_dim(out, partner_block, source, axis=0)
+    return in_order(out, concat_dim)
 
 
 def from_behind(value, axis, steps):
@@ -99,9 +123,7 @@
     sig_re, sig_im = lane_forward(signal_block, twiddle_re, twiddle_im)
     fil_re, fil_im = lane_forward(filter_block, twiddle_re, twiddle_im)
     signal_block, filter_block = (
-        lax.all_to_all(
-            jnp.stack([sig_re, sig_im], axis=2), "seq", split_axis=0, concat_axis=1, tiled=True
-        ),
+        sent_to_each(jnp.stack([sig_re, sig_im], axis=2), "seq", 0, 1),
         lax.all_to_all(
             jnp.stack([fil_re, fil_im], axis=2), "seq", split_axis=0, concat_axis=1, tiled=True
         ),

time: 2010 us -> 2080 us (1.035)
  starting transfers between devices: 43.1 us -> 228 us
  waiting for transfers between devices: 1060 us -> 919 us
  local copies, waits for them, and re-layouts: 157 us -> 182 us
    all_to_all x1 -> x0, waiting for transfers between devices: 353 us -> none  [per_device(): lax.all_to_all(jnp.stack([sig_re, sig_im], axis=2), 'seq', split_axis=0,...]
    ppermute x0 -> x7, starting transfers between devices: none -> 192 us  [sent_to_each(): lax.ppermute(sent, axis, [(i, (i + hop) % devices) for i in range(devices)])]
    all_to_all x1, waiting for transfers between devices: 0.01 us -> 126 us  [per_device(): lax.all_to_all(jnp.stack([fil_re, fil_im], axis=2), 'seq', split_axis=0,...]
    ppermute x0 -> x7, waiting for transfers between devices: none -> 85.8 us  [sent_to_each(): lax.ppermute(sent, axis, [(i, (i + hop) % devices) for i in range(devices)])]
  transfers between devices with their start and end apart: 8 -> 14, of which waited for: 3 -> 5; matrix products, arithmetic and copies ran while one was open for 11% -> 7% of each run, Pallas kernels for 0% -> 0%
where the time goes in v1:
time: 2080 us; the launch traced here: 2070 us
  waiting for transfers between devices  919 us (44%)
  blocking collectives  369 us (18%)
  matrix products  252 us (12%)
  starting transfers between devices  228 us (11%)
  local copies, waits for them, and re-layouts  182 us (9%)
  other arithmetic  119 us (6%)
    all_to_all x1, blocking collectives, per_device(): lax.all_to_all(jnp.stack([back_re, back_im], axis=2), 'seq', split_axis=1...  369 us
    ppermute x3, waiting for transfers between devices, from_behind(): lax.ppermute(value, axis, [(source, source + steps) for source in range(i...  356 us
    all_to_all x1, waiting for transfers between devices, per_device(): lax.all_to_all(signal_block, 'seq', split_axis=1, concat_axis=0, tiled=True)  351 us
    ppermute x7, starting transfers between devices, sent_to_each(): lax.ppermute(sent, axis, [(i, (i + hop) % devices) for i in range(devices)])  192 us
    all_to_all x1, waiting for transfers between devices, per_device(): lax.all_to_all(jnp.stack([fil_re, fil_im], axis=2), 'seq', split_axis=0,...  126 us
    ppermute x7, waiting for transfers between devices, sent_to_each(): lax.ppermute(sent, axis, [(i, (i + hop) % devices) for i in range(devices)])  85.8 us
    dot_general x6, matrix products, complex_apply(): product(matrix_re, data_im) + product(matrix_im, data_re)  70.4 us
    dot_general x6, matrix products, complex_apply(): product(matrix_im, data_im)  64.3 us
  transfers between devices with their start and end apart: 14, of which 5 were waited for; matrix products, arithmetic and copies ran while one was open for 7% of the time, Pallas kernels for 0%

profile of v1, /device:TPU:20, one launch (start us, length us, event | category | flops | bytes accessed | tf_op | source)
XLA Modules:
  0.0 2069.3 jit_solution(17651047371941265431)
XLA Ops:
  0.7 3.4 collective-permute-start.1
  4.8 3.4 collective-permute-start.2
  10.1 5.1 all-to-all-start.1
  16.9 10.3 maximum_convert_fusion.1
  27.2 6.3 maximum_convert_fusion.2
  33.5 39.5 %fusion.1 = f32[8192,512]{1,0:T(8,128)} fusion(f32[8194,512]{1,0:T(8,128)} %maximum_convert_fusion.2, f32[8194,512]{1,0:T(8,128)} %maximum_convert_fusion.1, f32[512]{0:T(512)S(1)} %bitcast.233, f32[512]{0:T(512)S(1)} %bitcast.234, f32[512]{0:T(512)S(1)} %bitcast.229, f32[512]{0:T(512)S(1)} %bitcast.230, f32[512]{0:T(512)S(1)} %bitcast.231, f32[512]{0:T(512)S(1)} %bitcast.232), kind=kLoop, calls=%fused_computation.2 | loop fusion | flops 46137344 | bytes 117452800 | tf_op jit(solution)/shard_map/mul | solution.py:109
  73.0 19.9 reshape.152
  92.9 17.7 copy.128
  110.6 6.5 all-to-all-start
  124.5 351.2 %all-to-all-done = f32[32,256,2,256]{3,0,2,1:T(8,128)} async-done(((f32[32,256,2,256]{3,0,2,1:T(8,128)}), f32[32,256,2,256]{3,0,2,1:T(8,128)}, u32[]{:S(2)}, u32[]{:S(2)}) %all-to-all-start) | async-done | bytes 16777248 | tf_op jit(solution)/shard_map/all_to_all | solution.py:118
  475.7 6.6 copy.130
  482.3 11.7 fusion.16
  494.0 11.8 fusion.17
  505.8 11.7 fusion.19
  517.5 21.9 %multiply_add_fusion.2 = (f32[256,32,256]{2,0,1:T(8,128)}, f32[256,32,256]{2,0,1:T(8,128)}) fusion(f32[256,32]{0,1:T(8,128)S(1)} %get-tuple-element.28, f32[256,32]{0,1:T(8,128)S(1)} %get-tuple-element.31, f32[256,32,256]{2,0,1:T(8,128)} %fusion.16, f32[256,32,256]{2,0,1:T(8,128)} %fusion.17, f32[256,32,256]{2,0,1:T(8,128)} %fusion.19, ...), kind=kOutput, calls=%fused_computation.46 | convolution fusion | flops 6460145664 | bytes 50397184 | tf_op jit(solution)/shard_map/kb,bam->kam/dot_general | solution.py:57
  539.4 8.2 copy_dynamic-update-slice_fusion.1
  547.6 8.8 copy_dynamic-update-slice_fusion
  556.4 5.7 copy-done
  564.0 45.9 %collective-permute-done.3 = f32[1,32,32,2,256]{4,2,0,3,1:T(8,128)} collective-permute-done((f32[1,32,32,2,256]{4,2,0,3,1:T(8,128)S(1)}, f32[1,32,32,2,256]{4,2,0,3,1:T(8,128)}, u32[]{:S(2)}, u32[]{:S(2)}) %collective-permute-start.3) | collective-permute-done | bytes 2097184 | tf_op jit(solution)/shard_map/ppermute | solution.py:32
  609.9 11.0 constant_dynamic-slice_fusion
  620.9 4.5 collective-permute-start.4
  631.9 39.9 %collective-permute-done.4 = f32[1,32,32,2,256]{4,2,0,3,1:T(8,128)S(1)} collective-permute-done((f32[1,32,32,2,256]{4,2,0,3,1:T(8,128)}, f32[1,32,32,2,256]{4,2,0,3,1:T(8,128)S(1)}, u32[]{:S(2)}, u32[]{:S(2)}) %collective-permute-start.4) | collective-permute-done | bytes 2097184 | tf_op jit(solution)/shard_map/ppermute | solution.py:32
  671.8 179.5 %collective-permute-start.9 = (f32[1,32,32,2,256]{4,2,0,3,1:T(8,128)S(1)}, f32[1,32,32,2,256]{4,2,0,3,1:T(8,128)}, u32[]{:S(2)}, u32[]{:S(2)}) collective-permute-start(f32[1,32,32,2,256]{4,2,0,3,1:T(8,128)S(1)} %get-tuple-element.9), channel_id=1, source_target_pairs={{0,7},{1,0},{2,1},{3,2},{4,3},{5,4},{6,5},{7,6},{8,15},{9,8},{10,9... | collective-permute-start | bytes 6291464 | tf_op jit(solution)/shard_map/ppermute | solution.py:32
  853.8 6.0 all-to-all-start.2
  859.9 125.8 %all-to-all-done.2 = f32[8,1,2048]{2,1,0:T(1,128)S(1)} async-done(((f32[8,1,2048]{2,1,0:T(1,128)}), f32[8,1,2048]{2,1,0:T(1,128)S(1)}, u32[]{:S(2)}, u32[]{:S(2)}) %all-to-all-start.2) | async-done | bytes 65568 | tf_op jit(solution)/shard_map/all_to_all | solution.py:127
  1011.2 19.7 fusion.20
  1031.0 18.0 fusion.21
  1049.0 18.3 fusion.23
  1067.3 25.7 %multiply_subtract_fusion.1 = (f32[32,256,256]{2,1,0:T(8,128)}, f32[32,256,256]{2,1,0:T(8,128)}) fusion(f32[32,256]{1,0:T(8,128)S(1)} %convolution_add_fusion, f32[32,256]{1,0:T(8,128)S(1)} %convolution_subtract_fusion, f32[32,256,256]{2,1,0:T(8,128)} %fusion.20, f32[32,256,256]{2,1,0:T(8,128)} %fusion.21, f32[32,256,256]{2,1,0:T(8,128)} %fusion.23, ...), kind=kOutput, calls=%fused_computation.45 | convolution fusion | flops 6460145664 | bytes 50397184 | tf_op jit(solution)/shard_map/ja,kam->kjm/dot_general | solution.py:57
  1093.1 13.5 fusion.10
  1106.5 7.7 fusion.8
  1114.2 11.5 subtract_bitcast_fusion
  1125.7 10.9 add_bitcast_fusion
  1136.6 9.8 pad_maximum_fusion
  1146.3 19.9 copy.152
  1166.2 368.6 %all_to_all.87 = f32[32,256,2,256]{3,0,2,1:T(8,128)S(1)} all-to-all(f32[32,256,2,256]{3,0,2,1:T(8,128)} %copy.152), channel_id=1, replica_groups=mesh['chan'=4,'seq'=8] {'seq'}, dimensions={1} | all-to-all | bytes 33554432 | tf_op jit(solution)/shard_map/all_to_all | solution.py:135
  1536.7 12.4 fusion.28
  1549.2 12.7 fusion.29
  1561.9 17.7 multiply_bitcast_fusion.1
  1579.6 16.1 multiply_bitcast_fusion
  1595.7 6.9 pad_maximum_fusion.1
  1602.5 20.2 copy.155
  1622.8 7.5 all-to-all-start.4
  1634.3 356.4 %collective-permute-done = bf16[2,512]{1,0:T(2,128)(2,1)S(1)} collective-permute-done((bf16[2,512]{1,0:T(2,128)(2,1)S(1)}, bf16[2,512]{1,0:T(2,128)(2,1)S(1)}, u32[]{:S(2)}, u32[]{:S(2)}) %collective-permute-start) | collective-permute-done | bytes 2080 | tf_op jit(solution)/shard_map/ppermute | solution.py:40
  1990.7 9.8 maximum_convert_fusion
  2000.5 27.6 %copy.156 = f32[32,8,32,2,256]{4,3,2,1,0:T(2,128)S(1)} copy(f32[32,8,32,2,256]{4,2,3,0,1:T(8,128)} %bitcast.62) | data formatting | bytes 33554432 | tf_op jit(solution)/shard_map/all_to_all | solution.py:139
  2028.2 7.2 copy.190
  2035.4 33.7 %fusion.6 = f32[8192,512]{1,0:T(8,128)} fusion(f32[8194,512]{1,0:T(8,128)} %maximum_convert_fusion, f32[8192,512]{1,0:T(8,128)} %bitcast.212, f32[8192,512]{1,0:T(8,128)} %fusion.1, f32[512]{0:T(512)S(1)} %copy-done.11, f32[512]{0:T(512)S(1)} %bitcast.227, f32[512]{0:T(512)S(1)} %bitcast.228, f32[512]{0:T(512)S(1)} %bitcast.226), kind=kLoop, calls=%fused_computation.13 | loop fusion | flops 33554432 | bytes 100671488 | tf_op jit(solution)/shard_map/mul | solution.py:143
  (86 shorter events, 54.5 us)
Async XLA Ops:
  0.7 16.1 collective-permute-start.1
  4.8 22.4 %collective-permute-start.2 = (bf16[2,512]{1,0:T(2,128)(2,1)S(1)}, bf16[2,512]{1,0:T(2,128)(2,1)S(1)}, u32[]{:S(2)}, u32[]{:S(2)}) collective-permute-start(bf16[2,512]{1,0:T(2,128)(2,1)S(1)} %slice.108), channel_id=1, source_target_pairs={{0,1},{1,2},{2,3},{3,4},{4,5},{5,6},{6,7},{8,9},{9,10},{10,11},{11... | collective-permute-start | bytes 6152 | tf_op jit(solution)/shard_map/ppermute | solution.py:40
  10.1 100.4 %all-to-all-start.1 = ((f32[8,1,2048]{2,1,0:T(1,128)}), f32[8,1,2048]{2,1,0:T(1,128)S(1)}, u32[]{:S(2)}, u32[]{:S(2)}) async-start(f32[8,1,2048]{2,1,0:T(1,128)} %reshape.162), calls=%async_computation.1 | async-start | bytes 131072 | tf_op jit(solution)/shard_map/all_to_all | solution.py:119
  15.3 11.9 slice-start.2
  16.8 10.4 slice-start.3
  110.6 365.1 %all-to-all-start = ((f32[32,256,2,256]{3,0,2,1:T(8,128)}), f32[32,256,2,256]{3,0,2,1:T(8,128)}, u32[]{:S(2)}, u32[]{:S(2)}) async-start(f32[32,256,2,256]{3,0,2,1:T(8,128)} %copy.128), calls=%async_computation | async-start | bytes 33554432 | tf_op jit(solution)/shard_map/all_to_all | solution.py:118
  482.3 23.5 %copy-start.3 = (f32[8,32,32,2,256]{4,1,0,2,3:T(8,128)}, f32[8,32,32,2,256]{4,1,0,2,3:T(8,128)S(1)}, u32[]{:S(2)}) copy-start(f32[8,32,32,2,256]{4,1,0,2,3:T(8,128)S(1)} %copy.130) | copy-start | bytes 50331652
  556.4 5.8 copy-start
  562.3 47.6 %collective-permute-start.3 = (f32[1,32,32,2,256]{4,2,0,3,1:T(8,128)S(1)}, f32[1,32,32,2,256]{4,2,0,3,1:T(8,128)}, u32[]{:S(2)}, u32[]{:S(2)}) collective-permute-start(f32[1,32,32,2,256]{4,2,0,3,1:T(8,128)S(1)} %constant_dynamic-slice_fusion.6), channel_id=1, source_target_pairs={{0,1},{1,2},{2,3},{3,4},{4,5},{5,6},{6,7},{7,0},{8,9},{9,10},{10,1... | collective-permute-start | bytes 6291464 | tf_op jit(solution)/shard_map/ppermute | solution.py:32
  620.9 50.9 %collective-permute-start.4 = (f32[1,32,32,2,256]{4,2,0,3,1:T(8,128)}, f32[1,32,32,2,256]{4,2,0,3,1:T(8,128)S(1)}, u32[]{:S(2)}, u32[]{:S(2)}) collective-permute-start(f32[1,32,32,2,256]{4,2,0,3,1:T(8,128)} %get-tuple-element.14), channel_id=1, source_target_pairs={{0,2},{1,3},{2,4},{3,5},{4,6},{5,7},{6,0},{7,1},{8,10},{9,11},{10,... | collective-permute-start | bytes 6291464 | tf_op jit(solution)/shard_map/ppermute | solution.py:32
  625.4 369.9 %collective-permute-start.5 = (f32[1,32,32,2,256]{4,2,0,3,1:T(8,128)}, f32[1,32,32,2,256]{4,2,0,3,1:T(8,128)}, u32[]{:S(2)}, u32[]{:S(2)}) collective-permute-start(f32[1,32,32,2,256]{4,2,0,3,1:T(8,128)} %get-tuple-element.13), channel_id=1, source_target_pairs={{0,3},{1,4},{2,5},{3,6},{4,7},{5,0},{6,1},{7,2},{8,11},{9,12},{10,... | collective-permute-start | bytes 6291464 | tf_op jit(solution)/shard_map/ppermute | solution.py:32
  625.9 372.6 %collective-permute-start.6 = (f32[1,32,32,2,256]{4,2,0,3,1:T(8,128)}, f32[1,32,32,2,256]{4,2,0,3,1:T(8,128)}, u32[]{:S(2)}, u32[]{:S(2)}) collective-permute-start(f32[1,32,32,2,256]{4,2,0,3,1:T(8,128)} %get-tuple-element.12), channel_id=1, source_target_pairs={{0,4},{1,5},{2,6},{3,7},{4,0},{5,1},{6,2},{7,3},{8,12},{9,13},{10,... | collective-permute-start | bytes 6291464 | tf_op jit(solution)/shard_map/ppermute | solution.py:32
  626.3 375.4 %collective-permute-start.7 = (f32[1,32,32,2,256]{4,2,0,3,1:T(8,128)}, f32[1,32,32,2,256]{4,2,0,3,1:T(8,128)}, u32[]{:S(2)}, u32[]{:S(2)}) collective-permute-start(f32[1,32,32,2,256]{4,2,0,3,1:T(8,128)} %get-tuple-element.11), channel_id=1, source_target_pairs={{0,5},{1,6},{2,7},{3,0},{4,1},{5,2},{6,3},{7,4},{8,13},{9,14},{10,... | collective-permute-start | bytes 6291464 | tf_op jit(solution)/shard_map/ppermute | solution.py:32
  629.2 375.7 %collective-permute-start.8 = (f32[1,32,32,2,256]{4,2,0,3,1:T(8,128)}, f32[1,32,32,2,256]{4,2,0,3,1:T(8,128)}, u32[]{:S(2)}, u32[]{:S(2)}) collective-permute-start(f32[1,32,32,2,256]{4,2,0,3,1:T(8,128)} %get-tuple-element.10), channel_id=1, source_target_pairs={{0,6},{1,7},{2,0},{3,1},{4,2},{5,3},{6,4},{7,5},{8,14},{9,15},{10,... | collective-permute-start | bytes 6291464 | tf_op jit(solution)/shard_map/ppermute | solution.py:32
  671.8 179.6 %copy-start.6 = (f32[1,32,32,2,256]{4,2,0,3,1:T(8,128)}, f32[1,32,32,2,256]{4,2,0,3,1:T(8,128)S(1)}, u32[]{:S(2)}) copy-start(f32[1,32,32,2,256]{4,2,0,3,1:T(8,128)S(1)} %collective-permute-done.4) | copy-start | bytes 6291460
  671.8 336.3 %collective-permute-start.9 = (f32[1,32,32,2,256]{4,2,0,3,1:T(8,128)S(1)}, f32[1,32,32,2,256]{4,2,0,3,1:T(8,128)}, u32[]{:S(2)}, u32[]{:S(2)}) collective-permute-start(f32[1,32,32,2,256]{4,2,0,3,1:T(8,128)S(1)} %get-tuple-element.9), channel_id=1, source_target_pairs={{0,7},{1,0},{2,1},{3,2},{4,3},{5,4},{6,5},{7,6},{8,15},{9,8},{10,9... | collective-permute-start | bytes 6291464 | tf_op jit(solution)/shard_map/ppermute | solution.py:32
  853.8 131.8 %all-to-all-start.2 = ((f32[8,1,2048]{2,1,0:T(1,128)}), f32[8,1,2048]{2,1,0:T(1,128)S(1)}, u32[]{:S(2)}, u32[]{:S(2)}) async-start(f32[8,1,2048]{2,1,0:T(1,128)} %reshape.164), calls=%async_computation.2 | async-start | bytes 131072 | tf_op jit(solution)/shard_map/all_to_all | solution.py:127
  1011.2 19.7 copy-start.1
  1093.0 13.5 copy-start.4
  1093.1 21.1 %slice-start = ((s8[8388608]{0:T(1024)(128)(4,1)}), s8[4194304]{0:T(1024)(128)(4,1)S(1)}, s32[]{:S(2)}) async-start(s8[8388608]{0:T(1024)(128)(4,1)} %bitcast.210), calls=%async_computation.5 | async-start | bytes 8388608
  1106.5 7.7 slice-start.1
  1534.9 1.9 copy-start.7
  1536.7 12.5 copy-start.2
  1561.9 17.7 copy-start.5
  1622.8 377.7 %all-to-all-start.4 = ((f32[256,32,2,256]{3,1,2,0:T(8,128)}), f32[256,32,2,256]{3,1,2,0:T(8,128)}, u32[]{:S(2)}, u32[]{:S(2)}) async-start(f32[256,32,2,256]{3,1,2,0:T(8,128)} %copy.155), calls=%async_computation.4 | async-start | bytes 33554432 | tf_op jit(solution)/shard_map/all_to_all | solution.py:139
  1631.0 359.7 %collective-permute-start = (bf16[2,512]{1,0:T(2,128)(2,1)S(1)}, bf16[2,512]{1,0:T(2,128)(2,1)S(1)}, u32[]{:S(2)}, u32[]{:S(2)}) collective-permute-start(bf16[2,512]{1,0:T(2,128)(2,1)S(1)} %slice.94), channel_id=1, source_target_pairs={{0,1},{1,2},{2,3},{3,4},{4,5},{5,6},{6,7},{8,9},{9,10},{10,11},{11... | collective-permute-start | bytes 6152 | tf_op jit(solution)/shard_map/ppermute | solution.py:40
  2028.1 7.3 copy-start.8
  2028.1 7.3 copy-start.9
  2028.1 7.3 copy-start.10
  2028.2 7.3 copy-start.11
